TPU v7x, 1024 devices: a whole 4x4x32 slice. The times are simulated.
1024 devices in a mesh: seq: 128 (over z, x), kvh: 8 (over y, core).
Axes of the slice: x: 4, y: 4, z: 32, core: 2. Of those that a mesh axis runs over, the one named last changes fastest.
Arguments:
- queries: bfloat16 [16384, 64, 128], P('seq', 'kvh'), may hold values from -160 to 160
- keys: bfloat16 [16384, 8, 128], P('seq', 'kvh'), may hold values from -4 to 4
- values: bfloat16 [16384, 8, 128], P('seq', 'kvh'), may hold values from -6 to 6
- output_gradient: bfloat16 [16384, 64, 128], P(('seq', 'kvh')), may hold values from -6 to 6
- doc_lengths: int32 [128], replicated, may hold values from 1 to 256, 16384 in all
- prefix_lengths: int32 [128], replicated, may hold values from 0 to 127
Outputs:
- grad_queries: bfloat16 [16384, 64, 128], P(('seq', 'kvh'))
- grad_keys: bfloat16 [16384, 8, 128], P('seq', 'kvh')
- grad_values: bfloat16 [16384, 8, 128], P('seq', 'kvh')
Inputs may be any that keep to these rules, and one draw needn't show every extreme that they name: `doc_lengths`: lengths sum to 16384; the longest document has exactly 256 tokens.
All inputs are finite; a program needn't handle non-finite values.
Results may differ from a plain program's by a relative error of at most 0.015.
Values may be sent and summed in bfloat16 or wider, within the bound.
A program may use at most 32 MiB of HBM per device.

v0:
```python
import jax
import jax.numpy as jnp
from jax import lax
from jax.sharding import PartitionSpec as P

BACK = 2


def shifted(block, axis, distance):
    devices = range(lax.axis_size(axis))
    route = [(i - distance, i) for i in devices if i - distance in devices]
    return lax.ppermute(block, axis, route)


def locate(positions, doc_end):
    return jnp.sum((positions[:, None] >= doc_end[None, :]).astype(jnp.int32), axis=1)


def scores_of(query_split, key_block, visible, score_scale):
    raw_scores = (
        jnp.einsum("tgqd,sgd->gqts", query_split, key_block, preferred_element_type=jnp.float32)
        * score_scale
    )
    return jnp.where(visible[None, None], raw_scores, -1e30)


def dprobs_of(cot_split, value_block):
    return jnp.einsum("tgqd,sgd->gqts", cot_split, value_block, preferred_element_type=jnp.float32)


def grads_of(probs, dprobs, row_delta, key_block, query_split, cot_split, score_scale):
    dscores = (probs * (dprobs - row_delta[..., None])).astype(jnp.bfloat16)
    probs_half = probs.astype(jnp.bfloat16)
    query_term = jnp.einsum(
        "gqts,sgd->tgqd", dscores, key_block, preferred_element_type=jnp.float32
    )
    key_term = (
        jnp.einsum("gqts,tgqd->sgd", dscores, query_split, preferred_element_type=jnp.float32)
        * score_scale
    )
    value_term = jnp.einsum(
        "gqts,tgqd->sgd", probs_half, cot_split, preferred_element_type=jnp.float32
    )
    return (query_term, key_term, value_term)


def local(queries, keys, values, output_gradient, doc_lengths, prefix_lengths):
    rows_dev, heads_dev, head_size = queries.shape
    kv_heads = keys.shape[1]
    group_size = heads_dev // kv_heads
    score_scale = head_size ** (-0.5)
    seq_count = lax.axis_size("seq")
    seq_index = lax.axis_index("seq")
    cotangent = lax.all_to_all(output_gradient, "kvh", split_axis=1, concat_axis=0, tiled=True)
    query_split = queries.reshape(rows_dev, kv_heads, group_size, head_size)
    cot_split = cotangent.reshape(rows_dev, kv_heads, group_size, head_size)
    doc_end = jnp.cumsum(doc_lengths)
    prefix_end = doc_end - doc_lengths + prefix_lengths
    doc_slots = jnp.arange(doc_lengths.shape[0], dtype=jnp.int32)
    local_rows = jnp.arange(rows_dev, dtype=jnp.int32)
    query_pos = seq_index * rows_dev + local_rows
    query_doc = locate(query_pos, doc_end)
    offsets = [0] + [back_by for back_by in range(1, BACK + 1)] + [-1]
    tiles = []
    for shift_by in offsets:
        if shift_by == 0:
            key_block, value_block = (keys, values)
        else:
            key_block, value_block = shifted((keys, values), "seq", shift_by)
        source_shard = seq_index - shift_by
        key_pos = source_shard * rows_dev + local_rows
        key_doc = locate(key_pos, doc_end)
        key_prefix = jnp.sum(
            jnp.where(key_doc[:, None] == doc_slots[None, :], prefix_end[None, :], 0), axis=1
        )
        inside = (source_shard >= 0) & (source_shard < seq_count)
        same_doc = query_doc[:, None] == key_doc[None, :]
        allowed = (key_pos[None, :] <= query_pos[:, None]) | (
            key_pos[None, :] < key_prefix[None, :]
        )
        visible = same_doc & allowed & inside
        tiles.append((key_block, value_block, visible, jnp.any(visible)))
    score_tiles = []
    row_max = None
    for key_block, value_block, visible, needed in tiles:
        tile_scores = scores_of(query_split, key_block, visible, score_scale)
        score_tiles.append(tile_scores)
        tile_max = jnp.max(tile_scores, axis=-1)
        row_max = tile_max if row_max is None else jnp.maximum(row_max, tile_max)
    expo_tiles = []
    row_sum = jnp.zeros(row_max.shape, jnp.float32)
    for number, tile_scores in enumerate(score_tiles):
        expo = jnp.where(
            tiles[number][2][None, None], jnp.exp(tile_scores - row_max[..., None]), 0.0
        )
        expo_tiles.append(expo)
        row_sum = row_sum + jnp.sum(expo, axis=-1)
    prob_tiles = []
    dprob_tiles = []
    row_delta = jnp.zeros(row_max.shape, jnp.float32)
    for number, expo in enumerate(expo_tiles):
        probs = expo / row_sum[..., None]
        value_block = tiles[number][1]
        dprobs = dprobs_of(cot_split, value_block)
        prob_tiles.append(probs)
        dprob_tiles.append(dprobs)
        row_delta = row_delta + jnp.sum(probs * dprobs, axis=-1)
    query_acc = jnp.zeros((rows_dev, kv_heads, group_size, head_size), jnp.float32)
    partial_list = []
    for number, probs in enumerate(prob_tiles):
        key_block = tiles[number][0]
        query_term, key_term, value_term = grads_of(
            probs, dprob_tiles[number], row_delta, key_block, query_split, cot_split, score_scale
        )
        query_acc = query_acc + query_term
        partial_list.append((key_term, value_term))
    keys_total, values_total = partial_list[0]
    for number, shift_by in enumerate(offsets):
        if shift_by != 0:
            got_keys, got_values = shifted(partial_list[number], "seq", -shift_by)
            keys_total = keys_total + got_keys
            values_total = values_total + got_values
    query_final = (
        (query_acc * score_scale).astype(jnp.bfloat16).reshape(rows_dev, heads_dev, head_size)
    )
    grad_queries = lax.all_to_all(query_final, "kvh", split_axis=0, concat_axis=1, tiled=True)
    return (grad_queries, keys_total.astype(jnp.bfloat16), values_total.astype(jnp.bfloat16))


def solution(mesh):
    in_specs = (
        P("seq", "kvh", None),
        P("seq", "kvh", None),
        P("seq", "kvh", None),
        P(("seq", "kvh"), None, None),
        P(),
        P(),
    )
    out_specs = (P(("seq", "kvh"), None, None), P("seq", "kvh", None), P("seq", "kvh", None))
    return jax.shard_map(local, mesh=mesh, in_specs=in_specs, out_specs=out_specs, check_vma=False)
```

profile of v0, /device:TPU:110, one launch (start us, length us, event | category | flops | bytes accessed | tf_op | source)
XLA Modules:
  0.0 79.8 jit_solution(812337408772954381)
XLA Ops:
  0.6 0.0 copy-start
  0.6 5.1 %collective-permute-start.3 = (bf16[128,1,128]{2,0,1:T(8,128)(2,1)}, bf16[128,1,128]{2,0,1:T(8,128)(2,1)S(1)}, u32[]{:S(2)}, u32[]{:S(2)}) collective-permute-start(bf16[128,1,128]{2,0,1:T(8,128)(2,1)} %param.8), channel_id=1, source_target_pairs={{0,8},{8,16},{16,24},{24,32},{32,40},{40,48},{48,56},{56,64},{64,7... | collective-permute-start | bytes 98312 | tf_op jit(solution)/shard_map/ppermute | solution.py:12
  5.7 1.9 %collective-permute-start.5 = (bf16[128,1,128]{2,0,1:T(8,128)(2,1)}, bf16[128,1,128]{2,0,1:T(8,128)(2,1)S(1)}, u32[]{:S(2)}, u32[]{:S(2)}) collective-permute-start(bf16[128,1,128]{2,0,1:T(8,128)(2,1)} %param.8), channel_id=1, source_target_pairs={{8,0},{16,8},{24,16},{32,24},{40,32},{48,40},{56,48},{64,56},{72,6... | collective-permute-start | bytes 98312 | tf_op jit(solution)/shard_map/ppermute | solution.py:12
  7.7 4.9 %collective-permute-start.4 = (bf16[128,1,128]{2,0,1:T(8,128)(2,1)}, bf16[128,1,128]{2,0,1:T(8,128)(2,1)S(1)}, u32[]{:S(2)}, u32[]{:S(2)}) collective-permute-start(bf16[128,1,128]{2,0,1:T(8,128)(2,1)} %param.8), channel_id=1, source_target_pairs={{0,16},{8,24},{16,32},{24,40},{32,48},{40,56},{48,64},{56,72},{64,... | collective-permute-start | bytes 98312 | tf_op jit(solution)/shard_map/ppermute | solution.py:12
  12.5 4.3 %collective-permute-start = (bf16[128,1,128]{2,0,1:T(8,128)(2,1)}, bf16[128,1,128]{2,0,1:T(8,128)(2,1)S(1)}, u32[]{:S(2)}, u32[]{:S(2)}) collective-permute-start(bf16[128,1,128]{2,0,1:T(8,128)(2,1)} %param.7), channel_id=1, source_target_pairs={{0,8},{8,16},{16,24},{24,32},{32,40},{40,48},{48,56},{56,64},{64,7... | collective-permute-start | bytes 98312 | tf_op jit(solution)/shard_map/ppermute | solution.py:12
  16.9 2.8 %collective-permute-start.2 = (bf16[128,1,128]{2,0,1:T(8,128)(2,1)}, bf16[128,1,128]{2,0,1:T(8,128)(2,1)S(1)}, u32[]{:S(2)}, u32[]{:S(2)}) collective-permute-start(bf16[128,1,128]{2,0,1:T(8,128)(2,1)} %param.7), channel_id=1, source_target_pairs={{8,0},{16,8},{24,16},{32,24},{40,32},{48,40},{56,48},{64,56},{72,6... | collective-permute-start | bytes 98312 | tf_op jit(solution)/shard_map/ppermute | solution.py:12
  19.6 1.8 %copy.44 = bf16[16,64,128]{2,0,1:T(8,128)(2,1)} copy(bf16[16,64,128]{2,1,0:T(8,128)(2,1)} %param.9) | data formatting | bytes 524288 | tf_op args[3]
  21.5 4.9 %all-to-all-start = ((bf16[16,64,128]{2,0,1:T(8,128)(2,1)}), bf16[16,64,128]{2,0,1:T(8,128)(2,1)S(1)}, u32[]{:S(2)}, u32[]{:S(2)}) async-start(bf16[16,64,128]{2,0,1:T(8,128)(2,1)} %copy.44), calls=%async_computation | async-start | bytes 524288 | tf_op jit(solution)/shard_map/all_to_all | solution.py:54
  26.4 0.7 copy-done.3
  27.0 0.1 copy.39
  27.1 0.2 reduce-window.8
  27.3 0.1 reduce.12
  27.4 0.0 copy-start.4
  27.5 0.6 copy-done.4
  28.1 0.1 convert_reduce_fusion.2
  28.2 0.1 select_reduce_fusion.2
  28.4 0.0 copy-start.1
  28.4 0.3 and_and_fusion.3
  28.7 0.5 copy-done.1
  29.2 0.2 fusion.80
  29.4 0.0 collective-permute-done
  29.4 4.1 %collective-permute-start.1 = (bf16[128,1,128]{2,0,1:T(8,128)(2,1)S(1)}, bf16[128,1,128]{2,0,1:T(8,128)(2,1)S(1)}, u32[]{:S(2)}, u32[]{:S(2)}) collective-permute-start(bf16[128,1,128]{2,0,1:T(8,128)(2,1)S(1)} %copy-done.1), channel_id=1, source_target_pairs={{0,16},{8,24},{16,32},{24,40},{32,48},{40,56},{48,64},{56,72},{64,... | collective-permute-start | bytes 98312 | tf_op jit(solution)/shard_map/ppermute | solution.py:12
  33.5 0.2 fusion.81
  33.8 2.9 %collective-permute-done.1 = bf16[128,1,128]{2,0,1:T(8,128)(2,1)S(1)} collective-permute-done((bf16[128,1,128]{2,0,1:T(8,128)(2,1)S(1)}, bf16[128,1,128]{2,0,1:T(8,128)(2,1)S(1)}, u32[]{:S(2)}, u32[]{:S(2)}) %collective-permute-start.1) | collective-permute-done | bytes 32800 | tf_op jit(solution)/shard_map/ppermute | solution.py:12
  36.7 0.2 fusion.79
  37.0 0.0 collective-permute-done.2
  37.0 0.2 fusion.78
  37.2 0.4 fusion.31
  37.7 0.0 all-to-all-done
  37.7 0.2 convolution_bitcast_fusion.4
  37.9 0.9 %convolution_bitcast_fusion.5 = f32[128,1,128]{2,0,1:T(8,128)} fusion(bf16[128,8,128]{2,0,1:T(8,128)(2,1)S(1)} %bitcast.250, f32[1,8,128,128]{2,3,1,0:T(8,128)S(1)} %get-tuple-element.30, f32[8,128]{1,0:T(8,128)S(1)} %add_add_fusion.1, f32[8,128]{1,0:T(8,128)S(1)} %maximum_maximum_fusion, pred[128,128]{0,1:T(8,128)(4,1)S(1)} %get-tuple-element.25), kind=kOutput, calls=%fused_computation.23 | convolution fusion | flops 34078720 | bytes 876544 | tf_op jit(solution)/shard_map/gqts,tgqd->sgd/dot_general | solution.py:41
  38.8 0.9 %convolution_bitcast_fusion.6 = f32[128,1,128]{2,0,1:T(8,128)} fusion(bf16[128,8,128]{2,0,1:T(8,128)(2,1)S(1)} %bitcast.251, f32[1,8,128,128]{2,3,1,0:T(8,128)S(1)} %get-tuple-element.34, f32[8,128]{1,0:T(8,128)S(1)} %add_add_fusion.1, f32[8,128]{1,0:T(8,128)S(1)} %maximum_maximum_fusion, pred[128,128]{0,1:T(8,128)(4,1)S(1)} %get-tuple-element.24), kind=kOutput, calls=%fused_computation.24 | convolution fusion | flops 34078720 | bytes 876544 | tf_op jit(solution)/shard_map/gqts,tgqd->sgd/dot_general | solution.py:41
  39.7 0.2 convolution_bitcast_fusion.3
  39.9 3.9 %collective-permute-start.9 = (f32[128,1,128]{2,0,1:T(8,128)}, f32[128,1,128]{2,0,1:T(8,128)S(1)}, u32[]{:S(2)}, u32[]{:S(2)}) collective-permute-start(f32[128,1,128]{2,0,1:T(8,128)} %convolution_bitcast_fusion.6), channel_id=1, source_target_pairs={{8,0},{16,8},{24,16},{32,24},{40,32},{48,40},{56,48},{64,56},{72,6... | collective-permute-start | bytes 196616 | tf_op jit(solution)/shard_map/ppermute | solution.py:12
  43.8 2.9 %collective-permute-start.10 = (f32[128,1,128]{2,0,1:T(8,128)}, f32[128,1,128]{2,0,1:T(8,128)}, u32[]{:S(2)}, u32[]{:S(2)}) collective-permute-start(f32[128,1,128]{2,0,1:T(8,128)} %convolution_bitcast_fusion.5), channel_id=1, source_target_pairs={{16,0},{24,8},{32,16},{40,24},{48,32},{56,40},{64,48},{72,56},{80,... | collective-permute-start | bytes 196616 | tf_op jit(solution)/shard_map/ppermute | solution.py:12
  46.7 0.0 collective-permute-done.5
  46.7 6.6 %collective-permute-start.11 = (f32[128,1,128]{2,0,1:T(8,128)S(1)}, f32[128,1,128]{2,0,1:T(8,128)}, u32[]{:S(2)}, u32[]{:S(2)}) collective-permute-start(f32[128,1,128]{2,0,1:T(8,128)S(1)} %convolution_bitcast_fusion.4), channel_id=1, source_target_pairs={{0,8},{8,16},{16,24},{24,32},{32,40},{40,48},{48,56},{56,64},{64,7... | collective-permute-start | bytes 196616 | tf_op jit(solution)/shard_map/ppermute | solution.py:12
  53.4 0.2 convolution_bitcast_fusion
  53.6 0.0 collective-permute-done.4
  53.6 0.2 convolution_bitcast_fusion.1
  53.8 0.0 collective-permute-done.3
  53.9 0.7 multiply_reduce_fusion.2
  54.6 0.6 fusion.38
  55.2 0.2 fusion.16
  55.4 0.2 fusion.18
  55.6 0.2 fusion.14
  55.8 2.8 %collective-permute-start.8 = (f32[128,1,128]{2,0,1:T(8,128)S(1)}, f32[128,1,128]{2,0,1:T(8,128)S(1)}, u32[]{:S(2)}, u32[]{:S(2)}) collective-permute-start(f32[128,1,128]{2,0,1:T(8,128)S(1)} %fusion.14), channel_id=1, source_target_pairs={{0,8},{8,16},{16,24},{24,32},{32,40},{40,48},{48,56},{56,64},{64,7... | collective-permute-start | bytes 196616 | tf_op jit(solution)/shard_map/ppermute | solution.py:12
  58.7 3.0 %collective-permute-start.6 = (f32[128,1,128]{2,0,1:T(8,128)S(1)}, f32[128,1,128]{2,0,1:T(8,128)S(1)}, u32[]{:S(2)}, u32[]{:S(2)}) collective-permute-start(f32[128,1,128]{2,0,1:T(8,128)S(1)} %fusion.18), channel_id=1, source_target_pairs={{8,0},{16,8},{24,16},{32,24},{40,32},{48,40},{56,48},{64,56},{72,6... | collective-permute-start | bytes 196616 | tf_op jit(solution)/shard_map/ppermute | solution.py:12
  61.7 0.3 fusion.67
  62.0 0.3 fusion.60
  62.2 0.3 convolution_add_fusion.1
  62.5 0.3 fusion.11
  62.8 0.9 %copy.50 = bf16[128,8,128]{2,1,0:T(8,128)(2,1)} copy(bf16[128,8,128]{2,0,1:T(8,128)(2,1)S(1)} %fusion.11) | data formatting | bytes 524288 | tf_op jit(solution)/shard_map/reshape | solution.py:124
  63.6 4.8 %all-to-all-start.1 = ((bf16[128,8,128]{2,1,0:T(8,128)(2,1)}), bf16[128,8,128]{2,1,0:T(8,128)(2,1)S(1)}, u32[]{:S(2)}, u32[]{:S(2)}) async-start(bf16[128,8,128]{2,1,0:T(8,128)(2,1)} %copy.50), calls=%async_computation.1 | async-start | bytes 524288 | tf_op jit(solution)/shard_map/all_to_all | solution.py:126
  68.5 0.0 collective-permute-done.9
  68.5 1.9 %collective-permute-start.7 = (f32[128,1,128]{2,0,1:T(8,128)S(1)}, f32[128,1,128]{2,0,1:T(8,128)S(1)}, u32[]{:S(2)}, u32[]{:S(2)}) collective-permute-start(f32[128,1,128]{2,0,1:T(8,128)S(1)} %fusion.16), channel_id=1, source_target_pairs={{16,0},{24,8},{32,16},{40,24},{48,32},{56,40},{64,48},{72,56},{80,... | collective-permute-start | bytes 196616 | tf_op jit(solution)/shard_map/ppermute | solution.py:12
  70.4 0.0 collective-permute-done.10
  70.4 0.0 collective-permute-done.11
  70.4 1.7 %fusion.27 = bf16[128,1,128]{2,0,1:T(8,128)(2,1)} fusion(f32[128,1,128]{2,0,1:T(8,128)} %collective-permute-done.11, f32[128,1,128]{2,0,1:T(8,128)} %collective-permute-done.10, f32[128,1,128]{2,0,1:T(8,128)S(1)} %collective-permute-done.9, bf16[128,8,128]{2,0,1:T(8,128)(2,1)S(1)} %bitcast.256, f32[1,8,128,128]{2,3,1,0:T(8,128)S(1)} %get-tuple-element.32, ...), kind=kOutput, calls=%fused_computation.45 | convolution fusion | flops 34144256 | bytes 1040384 | tf_op jit(solution)/shard_map/gqts,tgqd->sgd/dot_general | solution.py:41
  72.1 0.0 collective-permute-done.8
  72.1 0.0 collective-permute-done.6
  72.1 6.1 %collective-permute-done.7 = f32[128,1,128]{2,0,1:T(8,128)S(1)} collective-permute-done((f32[128,1,128]{2,0,1:T(8,128)S(1)}, f32[128,1,128]{2,0,1:T(8,128)S(1)}, u32[]{:S(2)}, u32[]{:S(2)}) %collective-permute-start.7) | collective-permute-done | bytes 65568 | tf_op jit(solution)/shard_map/ppermute | solution.py:12
  78.2 0.8 %fusion.26 = bf16[128,1,128]{2,0,1:T(8,128)(2,1)} fusion(f32[128,1,128]{2,0,1:T(8,128)S(1)} %collective-permute-done.8, f32[128,1,128]{2,0,1:T(8,128)S(1)} %collective-permute-done.7, f32[128,1,128]{2,0,1:T(8,128)S(1)} %collective-permute-done.6, bf16[8,128,128]{1,2,0:T(8,128)(2,1)S(1)} %get-tuple-element.22, bf16[128,8,128]{2,1,0:T(8,128)(2,1)S(1)} %copy-done), kind=kOutput, calls=%fused_computation.44 | convolution fusion | flops 33636352 | bytes 753664 | tf_op jit(solution)/shard_map/gqts,tgqd->sgd/dot_general | solution.py:38
  79.1 0.8 copy.85
  (16 shorter events, 0.1 us)
Async XLA Ops:
  0.6 28.1 %copy-start = (bf16[128,8,128]{2,1,0:T(8,128)(2,1)S(1)}, bf16[128,8,128]{2,1,0:T(8,128)(2,1)}, u32[]{:S(2)}) copy-start(bf16[128,8,128]{2,1,0:T(8,128)(2,1)} %param.6) | copy-start | bytes 786436
  0.6 53.2 %collective-permute-start.3 = (bf16[128,1,128]{2,0,1:T(8,128)(2,1)}, bf16[128,1,128]{2,0,1:T(8,128)(2,1)S(1)}, u32[]{:S(2)}, u32[]{:S(2)}) collective-permute-start(bf16[128,1,128]{2,0,1:T(8,128)(2,1)} %param.8), channel_id=1, source_target_pairs={{0,8},{8,16},{16,24},{24,32},{32,40},{40,48},{48,56},{56,64},{64,7... | collective-permute-start | bytes 98312 | tf_op jit(solution)/shard_map/ppermute | solution.py:12
  5.7 41.0 %collective-permute-start.5 = (bf16[128,1,128]{2,0,1:T(8,128)(2,1)}, bf16[128,1,128]{2,0,1:T(8,128)(2,1)S(1)}, u32[]{:S(2)}, u32[]{:S(2)}) collective-permute-start(bf16[128,1,128]{2,0,1:T(8,128)(2,1)} %param.8), channel_id=1, source_target_pairs={{8,0},{16,8},{24,16},{32,24},{40,32},{48,40},{56,48},{64,56},{72,6... | collective-permute-start | bytes 98312 | tf_op jit(solution)/shard_map/ppermute | solution.py:12
  7.7 45.9 %collective-permute-start.4 = (bf16[128,1,128]{2,0,1:T(8,128)(2,1)}, bf16[128,1,128]{2,0,1:T(8,128)(2,1)S(1)}, u32[]{:S(2)}, u32[]{:S(2)}) collective-permute-start(bf16[128,1,128]{2,0,1:T(8,128)(2,1)} %param.8), channel_id=1, source_target_pairs={{0,16},{8,24},{16,32},{24,40},{32,48},{40,56},{48,64},{56,72},{64,... | collective-permute-start | bytes 98312 | tf_op jit(solution)/shard_map/ppermute | solution.py:12
  12.5 16.9 %collective-permute-start = (bf16[128,1,128]{2,0,1:T(8,128)(2,1)}, bf16[128,1,128]{2,0,1:T(8,128)(2,1)S(1)}, u32[]{:S(2)}, u32[]{:S(2)}) collective-permute-start(bf16[128,1,128]{2,0,1:T(8,128)(2,1)} %param.7), channel_id=1, source_target_pairs={{0,8},{8,16},{16,24},{24,32},{32,40},{40,48},{48,56},{56,64},{64,7... | collective-permute-start | bytes 98312 | tf_op jit(solution)/shard_map/ppermute | solution.py:12
  16.9 20.1 %collective-permute-start.2 = (bf16[128,1,128]{2,0,1:T(8,128)(2,1)}, bf16[128,1,128]{2,0,1:T(8,128)(2,1)S(1)}, u32[]{:S(2)}, u32[]{:S(2)}) collective-permute-start(bf16[128,1,128]{2,0,1:T(8,128)(2,1)} %param.7), channel_id=1, source_target_pairs={{8,0},{16,8},{24,16},{32,24},{40,32},{48,40},{56,48},{64,56},{72,6... | collective-permute-start | bytes 98312 | tf_op jit(solution)/shard_map/ppermute | solution.py:12
  21.5 16.2 %all-to-all-start = ((bf16[16,64,128]{2,0,1:T(8,128)(2,1)}), bf16[16,64,128]{2,0,1:T(8,128)(2,1)S(1)}, u32[]{:S(2)}, u32[]{:S(2)}) async-start(bf16[16,64,128]{2,0,1:T(8,128)(2,1)} %copy.44), calls=%async_computation | async-start | bytes 524288 | tf_op jit(solution)/shard_map/all_to_all | solution.py:54
  26.4 0.7 copy-start.3
  27.4 0.7 copy-start.4
  28.4 0.8 copy-start.1
  29.4 7.3 %collective-permute-start.1 = (bf16[128,1,128]{2,0,1:T(8,128)(2,1)S(1)}, bf16[128,1,128]{2,0,1:T(8,128)(2,1)S(1)}, u32[]{:S(2)}, u32[]{:S(2)}) collective-permute-start(bf16[128,1,128]{2,0,1:T(8,128)(2,1)S(1)} %copy-done.1), channel_id=1, source_target_pairs={{0,16},{8,24},{16,32},{24,40},{32,48},{40,56},{48,64},{56,72},{64,... | collective-permute-start | bytes 98312 | tf_op jit(solution)/shard_map/ppermute | solution.py:12
  38.8 0.9 %copy-start.2 = (bf16[128,1,128]{2,0,1:T(8,128)(2,1)S(1)}, bf16[128,1,128]{2,0,1:T(8,128)(2,1)}, u32[]{:S(2)}) copy-start(bf16[128,1,128]{2,0,1:T(8,128)(2,1)} %param.8) | copy-start | bytes 98308
  39.9 28.6 %collective-permute-start.9 = (f32[128,1,128]{2,0,1:T(8,128)}, f32[128,1,128]{2,0,1:T(8,128)S(1)}, u32[]{:S(2)}, u32[]{:S(2)}) collective-permute-start(f32[128,1,128]{2,0,1:T(8,128)} %convolution_bitcast_fusion.6), channel_id=1, source_target_pairs={{8,0},{16,8},{24,16},{32,24},{40,32},{48,40},{56,48},{64,56},{72,6... | collective-permute-start | bytes 196616 | tf_op jit(solution)/shard_map/ppermute | solution.py:12
  43.8 26.6 %collective-permute-start.10 = (f32[128,1,128]{2,0,1:T(8,128)}, f32[128,1,128]{2,0,1:T(8,128)}, u32[]{:S(2)}, u32[]{:S(2)}) collective-permute-start(f32[128,1,128]{2,0,1:T(8,128)} %convolution_bitcast_fusion.5), channel_id=1, source_target_pairs={{16,0},{24,8},{32,16},{40,24},{48,32},{56,40},{64,48},{72,56},{80,... | collective-permute-start | bytes 196616 | tf_op jit(solution)/shard_map/ppermute | solution.py:12
  46.7 23.7 %collective-permute-start.11 = (f32[128,1,128]{2,0,1:T(8,128)S(1)}, f32[128,1,128]{2,0,1:T(8,128)}, u32[]{:S(2)}, u32[]{:S(2)}) collective-permute-start(f32[128,1,128]{2,0,1:T(8,128)S(1)} %convolution_bitcast_fusion.4), channel_id=1, source_target_pairs={{0,8},{8,16},{16,24},{24,32},{32,40},{40,48},{48,56},{56,64},{64,7... | collective-permute-start | bytes 196616 | tf_op jit(solution)/shard_map/ppermute | solution.py:12
  55.8 16.3 %collective-permute-start.8 = (f32[128,1,128]{2,0,1:T(8,128)S(1)}, f32[128,1,128]{2,0,1:T(8,128)S(1)}, u32[]{:S(2)}, u32[]{:S(2)}) collective-permute-start(f32[128,1,128]{2,0,1:T(8,128)S(1)} %fusion.14), channel_id=1, source_target_pairs={{0,8},{8,16},{16,24},{24,32},{32,40},{40,48},{48,56},{56,64},{64,7... | collective-permute-start | bytes 196616 | tf_op jit(solution)/shard_map/ppermute | solution.py:12
  58.7 13.5 %collective-permute-start.6 = (f32[128,1,128]{2,0,1:T(8,128)S(1)}, f32[128,1,128]{2,0,1:T(8,128)S(1)}, u32[]{:S(2)}, u32[]{:S(2)}) collective-permute-start(f32[128,1,128]{2,0,1:T(8,128)S(1)} %fusion.18), channel_id=1, source_target_pairs={{8,0},{16,8},{24,16},{32,24},{40,32},{48,40},{56,48},{64,56},{72,6... | collective-permute-start | bytes 196616 | tf_op jit(solution)/shard_map/ppermute | solution.py:12
  63.6 15.4 %all-to-all-start.1 = ((bf16[128,8,128]{2,1,0:T(8,128)(2,1)}), bf16[128,8,128]{2,1,0:T(8,128)(2,1)S(1)}, u32[]{:S(2)}, u32[]{:S(2)}) async-start(bf16[128,8,128]{2,1,0:T(8,128)(2,1)} %copy.50), calls=%async_computation.1 | async-start | bytes 524288 | tf_op jit(solution)/shard_map/all_to_all | solution.py:126
  68.5 9.8 %collective-permute-start.7 = (f32[128,1,128]{2,0,1:T(8,128)S(1)}, f32[128,1,128]{2,0,1:T(8,128)S(1)}, u32[]{:S(2)}, u32[]{:S(2)}) collective-permute-start(f32[128,1,128]{2,0,1:T(8,128)S(1)} %fusion.16), channel_id=1, source_target_pairs={{16,0},{24,8},{32,16},{40,24},{48,32},{56,40},{64,48},{72,56},{80,... | collective-permute-start | bytes 196616 | tf_op jit(solution)/shard_map/ppermute | solution.py:12
where the time goes:
time: 80.6 us; the launch traced here: 79.8 us
  starting transfers between devices  54 us (67%)
  waiting for transfers between devices  9.04 us (11%)
  matrix products  8.55 us (11%)
  local copies, waits for them, and re-layouts  5.37 us (7%)
  other arithmetic  1.84 us (2%)
  between operations  1.05 us (1%)
    ppermute x12, starting transfers between devices, shifted(): return lax.ppermute(block, axis, route)  44.3 us
    ppermute x12, waiting for transfers between devices, shifted(): return lax.ppermute(block, axis, route)  9.04 us
    all_to_all x1, starting transfers between devices, local(): lax.all_to_all(output_gradient, 'kvh', split_axis=1, concat_axis=0, tiled...  4.92 us
    all_to_all x1, starting transfers between devices, local(): lax.all_to_all(query_final, 'kvh', split_axis=0, concat_axis=1, tiled=True)  4.81 us
    dot_general x4, matrix products, grads_of(): jnp.einsum('gqts,tgqd->sgd', probs_half, cot_split, preferred_element_typ...  3.7 us
    unnamed x11, local copies, waits for them, and re-layouts  3.59 us
  transfers between devices with their start and end apart: 14, of which 2 were waited for; matrix products, arithmetic and copies ran while one was open for 17% of the time, Pallas kernels for 0%

commit v1 on v0

v1 whole, which is shorter than its diff:
```python
import functools

import jax
import jax.numpy as jnp
from jax import lax
from jax.experimental import pallas as pl
from jax.experimental.pallas import tpu as pltpu
from jax.sharding import PartitionSpec as P

MESH = pl.DeviceIdType.MESH
GROUP = 8
TILES = 4
LOG2E = 1.4426950408889634
NT = (((1,), (1,)), ((), ()))


def key_interval(positions, doc_len, doc_prefix, doc_start):
    start = jnp.max(jnp.where(doc_start <= positions, doc_start, 0), axis=0, keepdims=True)
    mine = doc_start == start
    length = jnp.sum(jnp.where(mine, doc_len, 0), axis=0, keepdims=True)
    prefix = jnp.sum(jnp.where(mine, doc_prefix, 0), axis=0, keepdims=True)
    stop = jnp.minimum(start + length, jnp.maximum(positions + 1, start + prefix))
    return start, stop


def kernel(
    n_seq, n_kvh, scale,
    q_hbm, k_hbm, v_hbm, og_hbm, len_hbm, pre_hbm,
    gq_out, gk_out, gv_out,
    qbuf, kbuf, vbuf, cot, lens, pres, q2, c2, probs, probs_half, dscores, gqbuf,
    part_out, part_in, own, final,
    local_sem, kv_send, kv_recv, cot_send, cot_recv, gq_send, gq_recv, part_send, part_recv, out_sem,
):
    seq = lax.axis_index("seq")
    me = lax.axis_index("kvh")
    chip = me // 2
    chips = n_kvh // 2
    partner = me + 1 - 2 * lax.rem(me, 2)
    rows = q2.shape[0]
    tokens = kbuf.shape[1]
    piece = rows // n_kvh
    width = 2 * piece

    def shard(distance):
        return lax.rem(seq + distance + n_seq, n_seq)

    barrier = pltpu.get_barrier_semaphore()
    others = [(seq, lax.rem(me + d, n_kvh)) for d in range(1, n_kvh)]
    others += [(shard(d), me) for d in (-2, -1, 1, 2)]
    for other in others:
        pl.semaphore_signal(barrier, inc=1, device_id=other, device_id_type=MESH)

    local = [
        pltpu.make_async_copy(len_hbm, lens, local_sem.at[0]),
        pltpu.make_async_copy(pre_hbm, pres, local_sem.at[1]),
        pltpu.make_async_copy(q_hbm, qbuf, local_sem.at[2]),
        pltpu.make_async_copy(k_hbm, kbuf.at[2], local_sem.at[3]),
        pltpu.make_async_copy(v_hbm, vbuf.at[2], local_sem.at[4]),
        pltpu.make_async_copy(og_hbm.at[:, me], cot.at[me], cot_recv.at[me]),
    ]
    for copy in local:
        copy.start()
    pl.semaphore_wait(barrier, len(others))

    sends = []
    for number, (distance, slot) in enumerate(((2, 0), (1, 1), (-1, 3))):
        copy = pltpu.make_async_remote_copy(
            k_hbm, kbuf.at[slot], kv_send.at[0, number], kv_recv.at[0, number],
            device_id=(shard(distance), me), device_id_type=MESH,
        )
        copy.start()
        sends.append(copy)
    targets = [2 * lax.rem(chip + d, chips) + core for d in (2, 1, 3) for core in (0, 1)]
    targets.append(partner)
    for number, target in enumerate(targets):
        copy = pltpu.make_async_remote_copy(
            og_hbm.at[:, target], cot.at[me], cot_send.at[number], cot_recv.at[me],
            device_id=(seq, target), device_id_type=MESH,
        )
        copy.start()
        sends.append(copy)
    for number, (distance, slot) in enumerate(((2, 0), (1, 1), (-1, 3))):
        copy = pltpu.make_async_remote_copy(
            v_hbm, vbuf.at[slot], kv_send.at[1, number], kv_recv.at[1, number],
            device_id=(shard(distance), me), device_id_type=MESH,
        )
        copy.start()
        sends.append(copy)

    local[0].wait()
    local[1].wait()
    docs = lens.shape[1]
    square = (docs, docs)
    by_sublane = lax.broadcasted_iota(jnp.int32, square, 0)
    by_lane = lax.broadcasted_iota(jnp.int32, square, 1)
    doc_len = jnp.transpose(jnp.broadcast_to(lens[...], square))
    doc_prefix = jnp.transpose(jnp.broadcast_to(pres[...], square))
    start_row = jnp.sum(jnp.where(by_sublane < by_lane, doc_len, 0), axis=0, keepdims=True)
    doc_start = jnp.transpose(jnp.broadcast_to(start_row, square))
    bounds = []
    for block in range(rows // docs):
        positions = seq * tokens + block * (docs // GROUP) + (by_lane[:1] >> 3)
        bounds.append(key_interval(positions, doc_len, doc_prefix, doc_start))

    local[2].wait()
    local[3].wait()
    for number in range(3):
        sends[number].wait_recv()
    k_all = kbuf[...].reshape(TILES * tokens, -1)
    key_pos = (seq - 2) * tokens + lax.broadcasted_iota(jnp.int32, (TILES * tokens, width), 0)
    per_chunk = width // docs
    for chunk in range(chips):
        at = pl.ds(chunk * width, width)
        block = qbuf[pl.ds(chunk * (width // GROUP), width // GROUP)].astype(jnp.float32)
        q_chunk = block.reshape(width, -1).astype(jnp.bfloat16)
        q2[at, :] = q_chunk
        low, high = (
            jnp.concatenate([b[side] for b in bounds[chunk * per_chunk:(chunk + 1) * per_chunk]], axis=1)
            for side in (0, 1)
        )
        scores = lax.dot_general(k_all, q_chunk, NT, preferred_element_type=jnp.float32)
        scores = jnp.where((key_pos >= low) & (key_pos < high), scores, -1e30)
        top = jnp.max(scores, axis=0, keepdims=True)
        expo = jnp.exp2((scores - top) * (scale * LOG2E))
        chunk_probs = expo * (1.0 / jnp.sum(expo, axis=0, keepdims=True))
        probs[:, at] = chunk_probs
        probs_half[:, at] = chunk_probs.astype(jnp.bfloat16)

    def send_parts(which, total):
        for number, (slot, distance) in enumerate(((0, -2), (1, -1), (3, 1))):
            part_out[which, number] = total[slot * tokens:(slot + 1) * tokens].astype(jnp.bfloat16)
            copy = pltpu.make_async_remote_copy(
                part_out.at[which, number], part_in.at[which, number],
                part_send.at[which, number], part_recv.at[which, number],
                device_id=(shard(distance), me), device_id_type=MESH,
            )
            copy.start()
            parts.append(copy)
        own[which] = total[2 * tokens:3 * tokens]

    parts = []
    for k in range(n_kvh):
        pltpu.make_async_copy(cot.at[k], cot.at[k], cot_recv.at[k]).wait()
        block = cot[k].astype(jnp.float32).reshape(piece, -1)
        c2[pl.ds(k * piece, piece), :] = block.astype(jnp.bfloat16)
    send_parts(0, jnp.dot(probs_half[...], c2[...], preferred_element_type=jnp.float32))

    local[4].wait()
    for number in range(3):
        sends[len(sends) - 3 + number].wait_recv()
    v_all = vbuf[...].reshape(TILES * tokens, -1)
    k_turned = jnp.transpose(k_all.astype(jnp.float32)).astype(jnp.bfloat16)
    queries = []
    for step, d in enumerate((2, 1, 3, 0)):
        target = lax.rem(chip + d, chips)
        at = pl.ds(pl.multiple_of(target * width, width), width)
        dprobs = lax.dot_general(v_all, c2[at, :], NT, preferred_element_type=jnp.float32)
        chunk_probs = probs[:, at]
        delta = jnp.sum(chunk_probs * dprobs, axis=0, keepdims=True)
        ds_chunk = (chunk_probs * (dprobs - delta)).astype(jnp.bfloat16)
        dscores[:, at] = ds_chunk
        turned = jnp.dot(k_turned, ds_chunk, preferred_element_type=jnp.float32)
        block = (jnp.transpose(turned) * scale).reshape(2, piece // GROUP, GROUP, -1)
        gqbuf[pl.ds(2 * target, 2)] = block.astype(jnp.bfloat16)
        if d == 0:
            copy = pltpu.make_async_copy(gqbuf.at[me], gq_out.at[:, me], gq_recv.at[me])
            copy.start()
            holders = [partner]
        else:
            holders = [2 * target, 2 * target + 1]
        for core, holder in enumerate(holders):
            copy = pltpu.make_async_remote_copy(
                gqbuf.at[holder], gq_out.at[:, me], gq_send.at[2 * step + core], gq_recv.at[me],
                device_id=(seq, holder), device_id_type=MESH,
            )
            copy.start()
            queries.append(copy)

    send_parts(1, jnp.dot(dscores[...], q2[...], preferred_element_type=jnp.float32) * scale)

    outs = []
    for which, out in ((0, gv_out), (1, gk_out)):
        total = own[which]
        for number in range(3):
            parts[3 * which + number].wait_recv()
            total = total + part_in[which, number].astype(jnp.float32)
        final[which] = total.astype(jnp.bfloat16)
        copy = pltpu.make_async_copy(final.at[which], out, out_sem.at[which])
        copy.start()
        outs.append(copy)
    for k in range(n_kvh):
        pltpu.make_async_copy(gqbuf.at[k], gq_out.at[:, k], gq_recv.at[k]).wait()
    for copy in sends + parts + queries:
        copy.wait_send()
    for copy in outs:
        copy.wait()


def solution(mesh):
    n_seq, n_kvh = mesh.shape["seq"], mesh.shape["kvh"]

    def step(queries, keys, values, output_gradient, doc_lengths, prefix_lengths):
        tokens, heads, size = queries.shape
        mine = output_gradient.shape[0]
        rows = tokens * heads
        bf16, f32, docs = jnp.bfloat16, jnp.float32, doc_lengths.shape[0]
        anywhere = pl.BlockSpec(memory_space=pl.ANY)
        dma = pltpu.SemaphoreType.DMA
        gq, gk, gv = pl.pallas_call(
            functools.partial(kernel, n_seq, n_kvh, size ** -0.5),
            out_shape=(
                jax.ShapeDtypeStruct((mine, n_kvh, heads, size), bf16),
                jax.ShapeDtypeStruct((tokens, size), bf16),
                jax.ShapeDtypeStruct((tokens, size), bf16),
            ),
            in_specs=[anywhere] * 6,
            out_specs=(anywhere,) * 3,
            scratch_shapes=[
                pltpu.VMEM((tokens, heads, size), bf16),
                pltpu.VMEM((TILES, tokens, size), bf16),
                pltpu.VMEM((TILES, tokens, size), bf16),
                pltpu.VMEM((n_kvh, mine, heads, size), bf16),
                pltpu.VMEM((1, docs), jnp.int32),
                pltpu.VMEM((1, docs), jnp.int32),
                pltpu.VMEM((rows, size), bf16),
                pltpu.VMEM((rows, size), bf16),
                pltpu.VMEM((TILES * tokens, rows), f32),
                pltpu.VMEM((TILES * tokens, rows), bf16),
                pltpu.VMEM((TILES * tokens, rows), bf16),
                pltpu.VMEM((n_kvh, mine, heads, size), bf16),
                pltpu.VMEM((2, 3, tokens, size), bf16),
                pltpu.VMEM((2, 3, tokens, size), bf16),
                pltpu.VMEM((2, tokens, size), f32),
                pltpu.VMEM((2, tokens, size), bf16),
                dma((5,)),
                dma((2, 3)),
                dma((2, 3)),
                dma((n_kvh,)),
                dma((n_kvh,)),
                dma((n_kvh,)),
                dma((n_kvh,)),
                dma((2, 3)),
                dma((2, 3)),
                dma((2,)),
            ],
            compiler_params=pltpu.CompilerParams(collective_id=0, has_side_effects=True),
        )(
            queries,
            keys.reshape(tokens, size),
            values.reshape(tokens, size),
            output_gradient.reshape(mine, n_kvh, heads, size),
            doc_lengths.reshape(1, docs),
            prefix_lengths.reshape(1, docs),
        )
        return gq.reshape(mine, n_kvh * heads, size), gk.reshape(tokens, 1, size), gv.reshape(tokens, 1, size)

    return jax.shard_map(
        step,
        mesh=mesh,
        in_specs=(P("seq", "kvh", None),) * 3 + (P(("seq", "kvh"), None, None), P(), P()),
        out_specs=(P(("seq", "kvh"), None, None), P("seq", "kvh", None), P("seq", "kvh", None)),
        check_vma=False,
    )
```

time: 80.6 us -> 40 us (0.50)
  the two profiles are of different devices: /device:TPU:110 before, /device:TPU:1 now
where the time goes in v1:
time: 40 us; the launch traced here: 39.2 us
  Pallas kernels  35.5 us (89%)
  local copies, waits for them, and re-layouts  3.06 us (8%)
  between operations  0.65 us (2%)
    pallas_call x1, Pallas kernels, step(): pl.pallas_call(functools.partial(kernel, n_seq, n_kvh, size ** (-0.5)), o...  35.5 us
    unnamed x7, local copies, waits for them, and re-layouts  3.06 us

profile of v1, /device:TPU:1, one launch (start us, length us, event | category | flops | bytes accessed | tf_op | source)
XLA Modules:
  0.0 39.2 jit_solution(8235707626676017754)
XLA Ops:
  0.6 35.5 %shard_map.85 = (bf16[16,8,8,128]{3,2,1,0:T(8,128)(2,1)}, bf16[128,128]{1,0:T(8,128)(2,1)}, bf16[128,128]{1,0:T(8,128)(2,1)}) custom-call(bf16[128,8,128]{2,1,0:T(8,128)(2,1)} %q_hbm.1, bf16[128,128]{1,0:T(8,128)(2,1)} %bitcast.10, bf16[128,128]{1,0:T(8,128)(2,1)} %bitcast.11, bf16[16,8,8,128]{3,2,1,0:T(8,128)(2,1)} %bitcast.8, s32[1,128]{1,0:T(1,128)} %bitcast.14, ...), custom_call_target="tpu_custom_call" | custom-call | tf_op jit(solution)/shard_map/pallas_call | solution.py:209
  36.2 0.0 copy-start.1
  36.2 1.7 %copy.12 = bf16[16,64,128]{2,1,0:T(8,128)(2,1)} copy(bf16[16,64,128]{2,1,0:T(8,128)(2,1)} %bitcast.9) | data formatting | bytes 524288
  37.8 0.0 copy-done.1
  37.8 0.0 copy-start
  37.9 0.6 %copy.13 = bf16[128,1,128]{2,0,1:T(8,128)(2,1)} copy(bf16[128,1,128]{2,0,1:T(8,128)(2,1)S(1)} %bitcast.13) | data formatting | bytes 65536
  38.5 0.2 copy-done
  38.6 0.6 %copy.14 = bf16[128,1,128]{2,0,1:T(8,128)(2,1)} copy(bf16[128,1,128]{2,0,1:T(8,128)(2,1)S(1)} %bitcast.12) | data formatting | bytes 65536
Async XLA Ops:
  36.2 1.7 %copy-start.1 = (bf16[128,128]{1,0:T(8,128)(2,1)S(1)}, bf16[128,128]{1,0:T(8,128)(2,1)}, u32[]{:S(2)}) copy-start(bf16[128,128]{1,0:T(8,128)(2,1)} %get-tuple-element.7) | copy-start | bytes 98308
  37.8 0.8 %copy-start = (bf16[128,128]{1,0:T(8,128)(2,1)S(1)}, bf16[128,128]{1,0:T(8,128)(2,1)}, u32[]{:S(2)}) copy-start(bf16[128,128]{1,0:T(8,128)(2,1)} %get-tuple-element.8) | copy-start | bytes 98308

commit v2 on v1

--- a/solution.py
+++ b/solution.py
@@ -41,14 +41,17 @@
     piece = rows // n_kvh
     width = 2 * piece
 
-    def shard(distance):
-        return lax.rem(seq + distance + n_seq, n_seq)
+    def inside(distance):
+        return (seq + distance >= 0) & (seq + distance < n_seq)
 
     barrier = pltpu.get_barrier_semaphore()
-    others = [(seq, lax.rem(me + d, n_kvh)) for d in range(1, n_kvh)]
-    others += [(shard(d), me) for d in (-2, -1, 1, 2)]
-    for other in others:
+    for d in range(1, n_kvh):
+        other = (seq, lax.rem(me + d, n_kvh))
         pl.semaphore_signal(barrier, inc=1, device_id=other, device_id_type=MESH)
+    for d in (-2, -1, 1, 2):
+        @pl.when(inside(d))
+        def _(d=d):
+            pl.semaphore_signal(barrier, inc=1, device_id=(seq + d, me), device_id_type=MESH)
 
     local = [
         pltpu.make_async_copy(len_hbm, lens, local_sem.at[0]),
@@ -60,16 +63,40 @@
     ]
     for copy in local:
         copy.start()
-    pl.semaphore_wait(barrier, len(others))
-
+    halo = ((2, 0), (1, 1), (-1, 3))
+    for number, (distance, slot) in enumerate(halo):
+        @pl.when(jnp.logical_not(inside(-distance)))
+        def _(slot=slot):
+            kbuf[slot] = jnp.zeros_like(kbuf[slot])
+            vbuf[slot] = jnp.zeros_like(vbuf[slot])
+
+        @pl.when(jnp.logical_not(inside(distance)))
+        def _(number=number):
+            part_in[:, number] = jnp.zeros_like(part_in[:, number])
+    pl.semaphore_wait(barrier, n_kvh - 1 + sum(inside(d).astype(jnp.int32) for d in (-2, -1, 1, 2)))
+
+    def halo_copy(which, number):
+        distance, slot = halo[number]
+        source, target = ((k_hbm, kbuf), (v_hbm, vbuf))[which]
+        return pltpu.make_async_remote_copy(
+            source, target.at[slot], kv_send.at[which, number], kv_recv.at[which, number],
+            device_id=(seq + distance, me), device_id_type=MESH,
+        )
+
+    def part_copy(which, number):
+        distance, _ = halo[number]
+        return pltpu.make_async_remote_copy(
+            part_out.at[which, number], part_in.at[which, number],
+            part_send.at[which, number], part_recv.at[which, number],
+            device_id=(seq - distance, me), device_id_type=MESH,
+        )
+
+    def each_halo(sign, act):
+        for number, (distance, _) in enumerate(halo):
+            pl.when(inside(sign * distance))(functools.partial(act, number))
+
+    each_halo(1, lambda number: halo_copy(0, number).start())
     sends = []
-    for number, (distance, slot) in enumerate(((2, 0), (1, 1), (-1, 3))):
-        copy = pltpu.make_async_remote_copy(
-            k_hbm, kbuf.at[slot], kv_send.at[0, number], kv_recv.at[0, number],
-            device_id=(shard(distance), me), device_id_type=MESH,
-        )
-        copy.start()
-        sends.append(copy)
     targets = [2 * lax.rem(chip + d, chips) + core for d in (2, 1, 3) for core in (0, 1)]
     targets.append(partner)
     for number, target in enumerate(targets):
@@ -79,13 +106,7 @@
         )
         copy.start()
         sends.append(copy)
-    for number, (distance, slot) in enumerate(((2, 0), (1, 1), (-1, 3))):
-        copy = pltpu.make_async_remote_copy(
-            v_hbm, vbuf.at[slot], kv_send.at[1, number], kv_recv.at[1, number],
-            device_id=(shard(distance), me), device_id_type=MESH,
-        )
-        copy.start()
-        sends.append(copy)
+    each_halo(1, lambda number: halo_copy(1, number).start())
 
     local[0].wait()
     local[1].wait()
@@ -104,8 +125,7 @@
 
     local[2].wait()
     local[3].wait()
-    for number in range(3):
-        sends[number].wait_recv()
+    each_halo(-1, lambda number: halo_copy(0, number).wait_recv())
     k_all = kbuf[...].reshape(TILES * tokens, -1)
     key_pos = (seq - 2) * tokens + lax.broadcasted_iota(jnp.int32, (TILES * tokens, width), 0)
     per_chunk = width // docs
@@ -127,18 +147,11 @@
         probs_half[:, at] = chunk_probs.astype(jnp.bfloat16)
 
     def send_parts(which, total):
-        for number, (slot, distance) in enumerate(((0, -2), (1, -1), (3, 1))):
+        for number, (_, slot) in enumerate(halo):
             part_out[which, number] = total[slot * tokens:(slot + 1) * tokens].astype(jnp.bfloat16)
-            copy = pltpu.make_async_remote_copy(
-                part_out.at[which, number], part_in.at[which, number],
-                part_send.at[which, number], part_recv.at[which, number],
-                device_id=(shard(distance), me), device_id_type=MESH,
-            )
-            copy.start()
-            parts.append(copy)
+        each_halo(-1, lambda number: part_copy(which, number).start())
         own[which] = total[2 * tokens:3 * tokens]
 
-    parts = []
     for k in range(n_kvh):
         pltpu.make_async_copy(cot.at[k], cot.at[k], cot_recv.at[k]).wait()
         block = cot[k].astype(jnp.float32).reshape(piece, -1)
@@ -146,8 +159,7 @@
     send_parts(0, jnp.dot(probs_half[...], c2[...], preferred_element_type=jnp.float32))
 
     local[4].wait()
-    for number in range(3):
-        sends[len(sends) - 3 + number].wait_recv()
+    each_halo(-1, lambda number: halo_copy(1, number).wait_recv())
     v_all = vbuf[...].reshape(TILES * tokens, -1)
     k_turned = jnp.transpose(k_all.astype(jnp.float32)).astype(jnp.bfloat16)
     queries = []
@@ -181,8 +193,8 @@
     outs = []
     for which, out in ((0, gv_out), (1, gk_out)):
         total = own[which]
+        each_halo(1, lambda number: part_copy(which, number).wait_recv())
         for number in range(3):
-            parts[3 * which + number].wait_recv()
             total = total + part_in[which, number].astype(jnp.float32)
         final[which] = total.astype(jnp.bfloat16)
         copy = pltpu.make_async_copy(final.at[which], out, out_sem.at[which])
@@ -190,7 +202,10 @@
         outs.append(copy)
     for k in range(n_kvh):
         pltpu.make_async_copy(gqbuf.at[k], gq_out.at[:, k], gq_recv.at[k]).wait()
-    for copy in sends + parts + queries:
+    for which in (0, 1):
+        each_halo(1, lambda number: halo_copy(which, number).wait_send())
+        each_halo(-1, lambda number: part_copy(which, number).wait_send())
+    for copy in sends + queries:
         copy.wait_send()
     for copy in outs:
         copy.wait()

time: 40 us -> 33.4 us (0.83)
  the two profiles are of different devices: /device:TPU:1 before, /device:TPU:6 now
where the time goes in v2:
time: 33.4 us; the launch traced here: 33.2 us
  Pallas kernels  29.5 us (88%)
  local copies, waits for them, and re-layouts  3.06 us (9%)
  between operations  0.65 us (2%)
    pallas_call x1, Pallas kernels, step(): pl.pallas_call(functools.partial(kernel, n_seq, n_kvh, size ** (-0.5)), o...  29.5 us
    unnamed x7, local copies, waits for them, and re-layouts  3.06 us

profile of v2, /device:TPU:6, one launch (start us, length us, event | category | flops | bytes accessed | tf_op | source)
XLA Modules:
  0.0 33.2 jit_solution(6914573533568174944)
XLA Ops:
  0.6 29.5 %shard_map.85 = (bf16[16,8,8,128]{3,2,1,0:T(8,128)(2,1)}, bf16[128,128]{1,0:T(8,128)(2,1)}, bf16[128,128]{1,0:T(8,128)(2,1)}) custom-call(bf16[128,8,128]{2,1,0:T(8,128)(2,1)} %q_hbm.1, bf16[128,128]{1,0:T(8,128)(2,1)} %bitcast.10, bf16[128,128]{1,0:T(8,128)(2,1)} %bitcast.11, bf16[16,8,8,128]{3,2,1,0:T(8,128)(2,1)} %bitcast.8, s32[1,128]{1,0:T(1,128)} %bitcast.14, ...), custom_call_target="tpu_custom_call" | custom-call | tf_op jit(solution)/shard_map/pallas_call | solution.py:224
  30.1 0.0 copy-start.1
  30.1 1.7 %copy.12 = bf16[16,64,128]{2,1,0:T(8,128)(2,1)} copy(bf16[16,64,128]{2,1,0:T(8,128)(2,1)} %bitcast.9) | data formatting | bytes 524288
  31.8 0.0 copy-done.1
  31.8 0.0 copy-start
  31.8 0.6 %copy.13 = bf16[128,1,128]{2,0,1:T(8,128)(2,1)} copy(bf16[128,1,128]{2,0,1:T(8,128)(2,1)S(1)} %bitcast.13) | data formatting | bytes 65536
  32.4 0.2 copy-done
  32.6 0.6 %copy.14 = bf16[128,1,128]{2,0,1:T(8,128)(2,1)} copy(bf16[128,1,128]{2,0,1:T(8,128)(2,1)S(1)} %bitcast.12) | data formatting | bytes 65536
Async XLA Ops:
  30.1 1.7 %copy-start.1 = (bf16[128,128]{1,0:T(8,128)(2,1)S(1)}, bf16[128,128]{1,0:T(8,128)(2,1)}, u32[]{:S(2)}) copy-start(bf16[128,128]{1,0:T(8,128)(2,1)} %get-tuple-element.7) | copy-start | bytes 98308
  31.8 0.8 %copy-start = (bf16[128,128]{1,0:T(8,128)(2,1)S(1)}, bf16[128,128]{1,0:T(8,128)(2,1)}, u32[]{:S(2)}) copy-start(bf16[128,128]{1,0:T(8,128)(2,1)} %get-tuple-element.8) | copy-start | bytes 98308

commit v3 on v2

--- a/solution.py
+++ b/solution.py
@@ -10,6 +10,7 @@
 MESH = pl.DeviceIdType.MESH
 GROUP = 8
 TILES = 4
+VMEM_LIMIT = 32 << 20
 LOG2E = 1.4426950408889634
 NT = (((1,), (1,)), ((), ()))
 
@@ -48,7 +49,7 @@
     for d in range(1, n_kvh):
         other = (seq, lax.rem(me + d, n_kvh))
         pl.semaphore_signal(barrier, inc=1, device_id=other, device_id_type=MESH)
-    for d in (-2, -1, 1, 2):
+    for d in (-2, -1):
         @pl.when(inside(d))
         def _(d=d):
             pl.semaphore_signal(barrier, inc=1, device_id=(seq + d, me), device_id_type=MESH)
@@ -73,7 +74,7 @@
         @pl.when(jnp.logical_not(inside(distance)))
         def _(number=number):
             part_in[:, number] = jnp.zeros_like(part_in[:, number])
-    pl.semaphore_wait(barrier, n_kvh - 1 + sum(inside(d).astype(jnp.int32) for d in (-2, -1, 1, 2)))
+    pl.semaphore_wait(barrier, n_kvh - 1 + sum(inside(d).astype(jnp.int32) for d in (1, 2)))
 
     def halo_copy(which, number):
         distance, slot = halo[number]
@@ -95,7 +96,8 @@
         for number, (distance, _) in enumerate(halo):
             pl.when(inside(sign * distance))(functools.partial(act, number))
 
-    each_halo(1, lambda number: halo_copy(0, number).start())
+    for number in (0, 1):
+        pl.when(inside(halo[number][0]))(lambda number=number: halo_copy(0, number).start())
     sends = []
     targets = [2 * lax.rem(chip + d, chips) + core for d in (2, 1, 3) for core in (0, 1)]
     targets.append(partner)
@@ -106,7 +108,8 @@
         )
         copy.start()
         sends.append(copy)
-    each_halo(1, lambda number: halo_copy(1, number).start())
+    for number in (0, 1):
+        pl.when(inside(halo[number][0]))(lambda number=number: halo_copy(1, number).start())
 
     local[0].wait()
     local[1].wait()
@@ -125,7 +128,14 @@
 
     local[2].wait()
     local[3].wait()
-    each_halo(-1, lambda number: halo_copy(0, number).wait_recv())
+
+    @pl.when(inside(-1))
+    def _():
+        halo_copy(0, 1).wait_recv()
+        halo_copy(0, 2).start()
+        halo_copy(1, 2).start()
+    for number in (0, 2):
+        pl.when(inside(-halo[number][0]))(lambda number=number: halo_copy(0, number).wait_recv())
     k_all = kbuf[...].reshape(TILES * tokens, -1)
     key_pos = (seq - 2) * tokens + lax.broadcasted_iota(jnp.int32, (TILES * tokens, width), 0)
     per_chunk = width // docs
@@ -211,6 +221,17 @@
         copy.wait()
 
 
+def finish(gq_in, gk_in, gv_in, gq_out, gk_out, gv_out, sem):
+    copies = [
+        pltpu.make_async_copy(source, target, sem.at[number])
+        for number, (source, target) in enumerate(((gq_in, gq_out), (gk_in, gk_out), (gv_in, gv_out)))
+    ]
+    for copy in copies:
+        copy.start()
+    for copy in copies:
+        copy.wait()
+
+
 def solution(mesh):
     n_seq, n_kvh = mesh.shape["seq"], mesh.shape["kvh"]
 
@@ -221,14 +242,15 @@
         bf16, f32, docs = jnp.bfloat16, jnp.float32, doc_lengths.shape[0]
         anywhere = pl.BlockSpec(memory_space=pl.ANY)
         dma = pltpu.SemaphoreType.DMA
-        gq, gk, gv = pl.pallas_call(
+        shapes = (
+            jax.ShapeDtypeStruct((mine, n_kvh, heads, size), bf16),
+            jax.ShapeDtypeStruct((tokens, size), bf16),
+            jax.ShapeDtypeStruct((tokens, size), bf16),
+        )
+        results = pl.pallas_call(
             functools.partial(kernel, n_seq, n_kvh, size ** -0.5),
-            out_shape=(
-                jax.ShapeDtypeStruct((mine, n_kvh, heads, size), bf16),
-                jax.ShapeDtypeStruct((tokens, size), bf16),
-                jax.ShapeDtypeStruct((tokens, size), bf16),
-            ),
-            in_specs=[anywhere] * 6,
+            out_shape=shapes,
+            in_specs=[pl.BlockSpec(memory_space=pltpu.HBM)] * 6,
             out_specs=(anywhere,) * 3,
             scratch_shapes=[
                 pltpu.VMEM((tokens, heads, size), bf16),
@@ -258,15 +280,23 @@
                 dma((2, 3)),
                 dma((2,)),
             ],
-            compiler_params=pltpu.CompilerParams(collective_id=0, has_side_effects=True),
-        )(
+            compiler_params=pltpu.CompilerParams(collective_id=0, has_side_effects=True, vmem_limit_bytes=VMEM_LIMIT),
+        )(*(pltpu.with_memory_space_constraint(x, pltpu.HBM) for x in (
             queries,
             keys.reshape(tokens, size),
             values.reshape(tokens, size),
             output_gradient.reshape(mine, n_kvh, heads, size),
             doc_lengths.reshape(1, docs),
             prefix_lengths.reshape(1, docs),
-        )
+        )))
+        gq, gk, gv = pl.pallas_call(
+            finish,
+            out_shape=shapes,
+            in_specs=[anywhere] * 3,
+            out_specs=(pl.BlockSpec(memory_space=pltpu.HBM),) * 3,
+            scratch_shapes=[dma((3,))],
+            compiler_params=pltpu.CompilerParams(vmem_limit_bytes=1 << 20),
+        )(*results)
         return gq.reshape(mine, n_kvh * heads, size), gk.reshape(tokens, 1, size), gv.reshape(tokens, 1, size)
 
     return jax.shard_map(

time: 33.4 us -> 33.5 us (level)
  the two profiles are of different devices: /device:TPU:6 before, /device:TPU:1 now
where the time goes in v3:
time: 33.5 us; the launch traced here: 33.4 us
  Pallas kernels  32.7 us (98%)
  between operations  0.64 us (2%)
    pallas_call x1, Pallas kernels, step(): pl.pallas_call(functools.partial(kernel, n_seq, n_kvh, size ** (-0.5)), o...  32 us
    pallas_call x1, Pallas kernels, step(): pl.pallas_call(finish, out_shape=shapes, in_specs=[anywhere] * 3, out_spe...  0.74 us

profile of v3, /device:TPU:1, one launch (start us, length us, event | category | flops | bytes accessed | tf_op | source)
XLA Modules:
  0.0 33.4 jit_solution(7874956499878843190)
XLA Ops:
  0.6 32.0 %shard_map.85 = (bf16[16,8,8,128]{3,2,1,0:T(8,128)(2,1)S(1)}, bf16[128,128]{1,0:T(8,128)(2,1)S(1)}, bf16[128,128]{1,0:T(8,128)(2,1)S(1)}) custom-call(bf16[128,8,128]{2,1,0:T(8,128)(2,1)} %q_hbm.1, bf16[128,128]{1,0:T(8,128)(2,1)} %bitcast.9, bf16[128,128]{1,0:T(8,128)(2,1)} %bitcast.10, bf16[16,8,8,128]{3,2,1,0:T(8,128)(2,1)} %bitcast.8, ...), custom_call_target="tpu_custom_call" | custom-call | tf_op jit(solution)/shard_map/pallas_call | solution.py:250
  32.6 0.7 %shard_map.86 = (bf16[16,8,8,128]{3,2,1,0:T(8,128)(2,1)}, bf16[128,128]{1,0:T(8,128)(2,1)}, bf16[128,128]{1,0:T(8,128)(2,1)}) custom-call(bf16[16,8,8,128]{3,2,1,0:T(8,128)(2,1)S(1)} %get-tuple-element.9.gq_in, bf16[128,128]{1,0:T(8,128)(2,1)S(1)} %get-tuple-element.10.gk_in, bf16[128,128]{1,0:T(8,128)(2,1)S(1)} %get-tuple-element.11.gv_in), custom_call_target="tpu_custom_call" | custom-call | tf_op jit(solution)/shard_map/pallas_call | solution.py:292

commit v4 on v3

--- a/solution.py
+++ b/solution.py
@@ -28,9 +28,9 @@
     n_seq, n_kvh, scale,
     q_hbm, k_hbm, v_hbm, og_hbm, len_hbm, pre_hbm,
     gq_out, gk_out, gv_out,
-    qbuf, kbuf, vbuf, cot, lens, pres, q2, c2, probs, probs_half, dscores, gqbuf,
+    qbuf, kbuf, vbuf, cot, lens, pres, q2, c2, probs, probs_half, gqbuf,
     part_out, part_in, own, final,
-    local_sem, kv_send, kv_recv, cot_send, cot_recv, gq_send, gq_recv, part_send, part_recv, out_sem,
+    local_sem, kv_send, kv_recv, cot_send, cot_recv, gq_send, gq_recv, part_send, part_recv, out_sem, ready,
 ):
     seq = lax.axis_index("seq")
     me = lax.axis_index("kvh")
@@ -96,6 +96,9 @@
         for number, (distance, _) in enumerate(halo):
             pl.when(inside(sign * distance))(functools.partial(act, number))
 
+    @pl.when(inside(1))
+    def _():
+        pl.semaphore_signal(ready, inc=1, device_id=(seq + 1, me), device_id_type=MESH)
     for number in (0, 1):
         pl.when(inside(halo[number][0]))(lambda number=number: halo_copy(0, number).start())
     sends = []
@@ -131,10 +134,10 @@
 
     @pl.when(inside(-1))
     def _():
-        halo_copy(0, 1).wait_recv()
+        pl.semaphore_wait(ready, 1)
         halo_copy(0, 2).start()
         halo_copy(1, 2).start()
-    for number in (0, 2):
+    for number in (0, 1, 2):
         pl.when(inside(-halo[number][0]))(lambda number=number: halo_copy(0, number).wait_recv())
     k_all = kbuf[...].reshape(TILES * tokens, -1)
     key_pos = (seq - 2) * tokens + lax.broadcasted_iota(jnp.int32, (TILES * tokens, width), 0)
@@ -156,40 +159,54 @@
         probs[:, at] = chunk_probs
         probs_half[:, at] = chunk_probs.astype(jnp.bfloat16)
 
-    def send_parts(which, total):
+    def store_parts(which, total):
         for number, (_, slot) in enumerate(halo):
             part_out[which, number] = total[slot * tokens:(slot + 1) * tokens].astype(jnp.bfloat16)
+        own[which] = total[2 * tokens:3 * tokens]
+
+    def send_parts(which):
         each_halo(-1, lambda number: part_copy(which, number).start())
-        own[which] = total[2 * tokens:3 * tokens]
-
+
+    local[4].wait()
+    each_halo(-1, lambda number: halo_copy(1, number).wait_recv())
     for k in range(n_kvh):
         pltpu.make_async_copy(cot.at[k], cot.at[k], cot_recv.at[k]).wait()
+    for k in range(n_kvh):
         block = cot[k].astype(jnp.float32).reshape(piece, -1)
         c2[pl.ds(k * piece, piece), :] = block.astype(jnp.bfloat16)
-    send_parts(0, jnp.dot(probs_half[...], c2[...], preferred_element_type=jnp.float32))
-
-    local[4].wait()
-    each_halo(-1, lambda number: halo_copy(1, number).wait_recv())
+
+    order = (2, 1, 3, 0)
     v_all = vbuf[...].reshape(TILES * tokens, -1)
     k_turned = jnp.transpose(k_all.astype(jnp.float32)).astype(jnp.bfloat16)
-    queries = []
-    for step, d in enumerate((2, 1, 3, 0)):
-        target = lax.rem(chip + d, chips)
-        at = pl.ds(pl.multiple_of(target * width, width), width)
+
+    def chunk_of(step):
+        target = lax.rem(chip + order[step], chips)
+        return target, pl.ds(pl.multiple_of(target * width, width), width)
+
+    def score_gradients(step):
+        _, at = chunk_of(step)
         dprobs = lax.dot_general(v_all, c2[at, :], NT, preferred_element_type=jnp.float32)
         chunk_probs = probs[:, at]
         delta = jnp.sum(chunk_probs * dprobs, axis=0, keepdims=True)
-        ds_chunk = (chunk_probs * (dprobs - delta)).astype(jnp.bfloat16)
-        dscores[:, at] = ds_chunk
+        return (chunk_probs * (dprobs - delta)).astype(jnp.bfloat16)
+
+    def query_gradients(step, ds_chunk):
+        target, _ = chunk_of(step)
         turned = jnp.dot(k_turned, ds_chunk, preferred_element_type=jnp.float32)
         block = (jnp.transpose(turned) * scale).reshape(2, piece // GROUP, GROUP, -1)
         gqbuf[pl.ds(2 * target, 2)] = block.astype(jnp.bfloat16)
-        if d == 0:
-            copy = pltpu.make_async_copy(gqbuf.at[me], gq_out.at[:, me], gq_recv.at[me])
-            copy.start()
-            holders = [partner]
-        else:
-            holders = [2 * target, 2 * target + 1]
+
+    def key_gradients(step, ds_chunk):
+        _, at = chunk_of(step)
+        return jnp.dot(ds_chunk, q2[at, :], preferred_element_type=jnp.float32)
+
+    queries = []
+
+    def send_queries(step):
+        target, _ = chunk_of(step)
+        holders = [2 * target, 2 * target + 1] if order[step] else [partner]
+        if not order[step]:
+            pltpu.make_async_copy(gqbuf.at[me], gq_out.at[:, me], gq_recv.at[me]).start()
         for core, holder in enumerate(holders):
             copy = pltpu.make_async_remote_copy(
                 gqbuf.at[holder], gq_out.at[:, me], gq_send.at[2 * step + core], gq_recv.at[me],
@@ -198,7 +215,20 @@
             copy.start()
             queries.append(copy)
 
-    send_parts(1, jnp.dot(dscores[...], q2[...], preferred_element_type=jnp.float32) * scale)
+    ds_chunk = score_gradients(0)
+    store_parts(0, jnp.dot(probs_half[...], c2[...], preferred_element_type=jnp.float32))
+    send_parts(0)
+    key_total = None
+    for step in range(chips):
+        later = score_gradients(step + 1) if step + 1 < chips else None
+        query_gradients(step, ds_chunk)
+        term = key_gradients(step, ds_chunk)
+        key_total = term if key_total is None else key_total + term
+        if later is None:
+            store_parts(1, key_total * scale)
+            send_parts(1)
+        send_queries(step)
+        ds_chunk = later
 
     outs = []
     for which, out in ((0, gv_out), (1, gk_out)):
@@ -263,7 +293,6 @@
                 pltpu.VMEM((rows, size), bf16),
                 pltpu.VMEM((TILES * tokens, rows), f32),
                 pltpu.VMEM((TILES * tokens, rows), bf16),
-                pltpu.VMEM((TILES * tokens, rows), bf16),
                 pltpu.VMEM((n_kvh, mine, heads, size), bf16),
                 pltpu.VMEM((2, 3, tokens, size), bf16),
                 pltpu.VMEM((2, 3, tokens, size), bf16),
@@ -279,6 +308,7 @@
                 dma((2, 3)),
                 dma((2, 3)),
                 dma((2,)),
+                pltpu.SemaphoreType.REGULAR,
             ],
             compiler_params=pltpu.CompilerParams(collective_id=0, has_side_effects=True, vmem_limit_bytes=VMEM_LIMIT),
         )(*(pltpu.with_memory_space_constraint(x, pltpu.HBM) for x in (

time: 33.5 us -> 29.8 us (0.89)
  Pallas kernels: 32.7 us -> 29 us
    pallas_call x1, Pallas kernels: 32 us -> 28.3 us  [step(): pl.pallas_call(functools.partial(kernel, n_seq, n_kvh, size ** (-0.5)), o...]
where the time goes in v4:
time: 29.8 us; the launch traced here: 29.7 us
  Pallas kernels  29 us (97%)
  between operations  0.64 us (2%)
    pallas_call x1, Pallas kernels, step(): pl.pallas_call(functools.partial(kernel, n_seq, n_kvh, size ** (-0.5)), o...  28.3 us
    pallas_call x1, Pallas kernels, step(): pl.pallas_call(finish, out_shape=shapes, in_specs=[anywhere] * 3, out_spe...  0.74 us

profile of v4, /device:TPU:1, one launch (start us, length us, event | category | flops | bytes accessed | tf_op | source)
XLA Modules:
  0.0 29.7 jit_solution(1024889546671868825)
XLA Ops:
  0.6 28.3 %shard_map.85 = (bf16[16,8,8,128]{3,2,1,0:T(8,128)(2,1)S(1)}, bf16[128,128]{1,0:T(8,128)(2,1)S(1)}, bf16[128,128]{1,0:T(8,128)(2,1)S(1)}) custom-call(bf16[128,8,128]{2,1,0:T(8,128)(2,1)} %q_hbm.1, bf16[128,128]{1,0:T(8,128)(2,1)} %bitcast.9, bf16[128,128]{1,0:T(8,128)(2,1)} %bitcast.10, bf16[16,8,8,128]{3,2,1,0:T(8,128)(2,1)} %bitcast.8, ...), custom_call_target="tpu_custom_call" | custom-call | tf_op jit(solution)/shard_map/pallas_call | solution.py:280
  28.9 0.7 %shard_map.86 = (bf16[16,8,8,128]{3,2,1,0:T(8,128)(2,1)}, bf16[128,128]{1,0:T(8,128)(2,1)}, bf16[128,128]{1,0:T(8,128)(2,1)}) custom-call(bf16[16,8,8,128]{3,2,1,0:T(8,128)(2,1)S(1)} %get-tuple-element.9.gq_in, bf16[128,128]{1,0:T(8,128)(2,1)S(1)} %get-tuple-element.10.gk_in, bf16[128,128]{1,0:T(8,128)(2,1)S(1)} %get-tuple-element.11.gv_in), custom_call_target="tpu_custom_call" | custom-call | tf_op jit(solution)/shard_map/pallas_call | solution.py:322

commit v5 on v4

--- a/solution.py
+++ b/solution.py
@@ -10,6 +10,7 @@
 MESH = pl.DeviceIdType.MESH
 GROUP = 8
 TILES = 4
+OWN = 1
 VMEM_LIMIT = 32 << 20
 LOG2E = 1.4426950408889634
 NT = (((1,), (1,)), ((), ()))
@@ -58,13 +59,13 @@
         pltpu.make_async_copy(len_hbm, lens, local_sem.at[0]),
         pltpu.make_async_copy(pre_hbm, pres, local_sem.at[1]),
         pltpu.make_async_copy(q_hbm, qbuf, local_sem.at[2]),
-        pltpu.make_async_copy(k_hbm, kbuf.at[2], local_sem.at[3]),
-        pltpu.make_async_copy(v_hbm, vbuf.at[2], local_sem.at[4]),
+        pltpu.make_async_copy(k_hbm, kbuf.at[OWN], local_sem.at[3]),
+        pltpu.make_async_copy(v_hbm, vbuf.at[OWN], local_sem.at[4]),
         pltpu.make_async_copy(og_hbm.at[:, me], cot.at[me], cot_recv.at[me]),
     ]
     for copy in local:
         copy.start()
-    halo = ((2, 0), (1, 1), (-1, 3))
+    halo = ((2, 2), (1, 0), (-1, 3))
     for number, (distance, slot) in enumerate(halo):
         @pl.when(jnp.logical_not(inside(-distance)))
         def _(slot=slot):
@@ -113,6 +114,12 @@
         sends.append(copy)
     for number in (0, 1):
         pl.when(inside(halo[number][0]))(lambda number=number: halo_copy(1, number).start())
+
+    @pl.when(inside(-1))
+    def _():
+        pl.semaphore_wait(ready, 1)
+        halo_copy(0, 2).start()
+        halo_copy(1, 2).start()
 
     local[0].wait()
     local[1].wait()
@@ -129,40 +136,70 @@
         positions = seq * tokens + block * (docs // GROUP) + (by_lane[:1] >> 3)
         bounds.append(key_interval(positions, doc_len, doc_prefix, doc_start))
 
+    tile = (tokens, width)
+    key_at = lax.broadcasted_iota(jnp.int32, tile, 0)
+    token_at = lax.broadcasted_iota(jnp.int32, tile, 1) >> 3
+    factor = scale * LOG2E
+
+    def is_back(chunk):
+        return key_at > token_at + chunk * (width // GROUP)
+
+    def hidden(scores, positions, bound):
+        return jnp.where((positions >= bound[0]) & (positions < bound[1]), scores, -1e30)
+
     local[2].wait()
     local[3].wait()
-
-    @pl.when(inside(-1))
-    def _():
-        pl.semaphore_wait(ready, 1)
-        halo_copy(0, 2).start()
-        halo_copy(1, 2).start()
-    for number in (0, 1, 2):
-        pl.when(inside(-halo[number][0]))(lambda number=number: halo_copy(0, number).wait_recv())
-    k_all = kbuf[...].reshape(TILES * tokens, -1)
-    key_pos = (seq - 2) * tokens + lax.broadcasted_iota(jnp.int32, (TILES * tokens, width), 0)
     per_chunk = width // docs
+    limits, tops, sums = [], [], []
     for chunk in range(chips):
         at = pl.ds(chunk * width, width)
         block = qbuf[pl.ds(chunk * (width // GROUP), width // GROUP)].astype(jnp.float32)
         q_chunk = block.reshape(width, -1).astype(jnp.bfloat16)
         q2[at, :] = q_chunk
-        low, high = (
+        limits.append([
             jnp.concatenate([b[side] for b in bounds[chunk * per_chunk:(chunk + 1) * per_chunk]], axis=1)
             for side in (0, 1)
-        )
-        scores = lax.dot_general(k_all, q_chunk, NT, preferred_element_type=jnp.float32)
-        scores = jnp.where((key_pos >= low) & (key_pos < high), scores, -1e30)
-        top = jnp.max(scores, axis=0, keepdims=True)
-        expo = jnp.exp2((scores - top) * (scale * LOG2E))
-        chunk_probs = expo * (1.0 / jnp.sum(expo, axis=0, keepdims=True))
-        probs[:, at] = chunk_probs
-        probs_half[:, at] = chunk_probs.astype(jnp.bfloat16)
+        ])
+        scores = lax.dot_general(kbuf[OWN], q_chunk, NT, preferred_element_type=jnp.float32)
+        scores = hidden(scores, key_at + seq * tokens, limits[chunk])
+        tops.append(jnp.max(scores, axis=0, keepdims=True))
+        expo = jnp.exp2((scores - tops[chunk]) * factor)
+        sums.append(jnp.sum(expo, axis=0, keepdims=True))
+        probs[OWN * tokens:(OWN + 1) * tokens, at] = expo
+
+    for number in (0, 1, 2):
+        pl.when(inside(-halo[number][0]))(lambda number=number: halo_copy(0, number).wait_recv())
+    k_all = kbuf[...].reshape(TILES * tokens, -1)
+    for chunk in range(chips):
+        at = pl.ds(chunk * width, width)
+        back = is_back(chunk)
+        before, _, far, ahead = (
+            lax.dot_general(kbuf[slot], q2[at, :], NT, preferred_element_type=jnp.float32) if slot != OWN else None
+            for slot in range(TILES)
+        )
+        before = hidden(before, key_at + (seq - 1) * tokens, limits[chunk])
+        outer = hidden(
+            jnp.where(back, far, ahead),
+            key_at + jnp.where(back, (seq - 2) * tokens, (seq + 1) * tokens),
+            limits[chunk],
+        )
+        top = jnp.maximum(tops[chunk], jnp.max(jnp.maximum(before, outer), axis=0, keepdims=True))
+        before = jnp.exp2((before - top) * factor)
+        outer = jnp.exp2((outer - top) * factor)
+        shrink = jnp.exp2((tops[chunk] - top) * factor)
+        inverse = 1.0 / (sums[chunk] * shrink + jnp.sum(before + outer, axis=0, keepdims=True))
+        before = before * inverse
+        outer = outer * inverse
+        middle = probs[OWN * tokens:(OWN + 1) * tokens, at] * (inverse * shrink)
+        for number, part in enumerate((before, middle, outer)):
+            probs[number * tokens:(number + 1) * tokens, at] = part
+        for slot, part in enumerate((before, middle, jnp.where(back, outer, 0.0), jnp.where(back, 0.0, outer))):
+            probs_half[slot * tokens:(slot + 1) * tokens, at] = part.astype(jnp.bfloat16)
 
     def store_parts(which, total):
         for number, (_, slot) in enumerate(halo):
             part_out[which, number] = total[slot * tokens:(slot + 1) * tokens].astype(jnp.bfloat16)
-        own[which] = total[2 * tokens:3 * tokens]
+        own[which] = total[OWN * tokens:(OWN + 1) * tokens]
 
     def send_parts(which):
         each_halo(-1, lambda number: part_copy(which, number).start())
@@ -184,11 +221,20 @@
         return target, pl.ds(pl.multiple_of(target * width, width), width)
 
     def score_gradients(step):
-        _, at = chunk_of(step)
+        target, at = chunk_of(step)
+        back = is_back(target)
         dprobs = lax.dot_general(v_all, c2[at, :], NT, preferred_element_type=jnp.float32)
-        chunk_probs = probs[:, at]
-        delta = jnp.sum(chunk_probs * dprobs, axis=0, keepdims=True)
-        return (chunk_probs * (dprobs - delta)).astype(jnp.bfloat16)
+        inner = dprobs[:2 * tokens]
+        outer = jnp.where(back, dprobs[2 * tokens:3 * tokens], dprobs[3 * tokens:])
+        inner_probs = probs[:2 * tokens, at]
+        outer_probs = probs[2 * tokens:, at]
+        delta = jnp.sum(inner_probs * inner, axis=0, keepdims=True)
+        delta = delta + jnp.sum(outer_probs * outer, axis=0, keepdims=True)
+        inner = (inner_probs * (inner - delta)).astype(jnp.bfloat16)
+        outer = outer_probs * (outer - delta)
+        far = jnp.where(back, outer, 0.0).astype(jnp.bfloat16)
+        ahead = jnp.where(back, 0.0, outer).astype(jnp.bfloat16)
+        return jnp.concatenate([inner, far, ahead], axis=0)
 
     def query_gradients(step, ds_chunk):
         target, _ = chunk_of(step)
@@ -291,7 +337,7 @@
                 pltpu.VMEM((1, docs), jnp.int32),
                 pltpu.VMEM((rows, size), bf16),
                 pltpu.VMEM((rows, size), bf16),
-                pltpu.VMEM((TILES * tokens, rows), f32),
+                pltpu.VMEM(((TILES - 1) * tokens, rows), f32),
                 pltpu.VMEM((TILES * tokens, rows), bf16),
                 pltpu.VMEM((n_kvh, mine, heads, size), bf16),
                 pltpu.VMEM((2, 3, tokens, size), bf16),

time: 29.8 us -> 29.8 us (level)
  no operation moved by 1% of the time
where the time goes in v5:
time: 29.8 us; the launch traced here: 29.6 us
  Pallas kernels  29 us (97%)
  between operations  0.64 us (2%)
    pallas_call x1, Pallas kernels, step(): pl.pallas_call(functools.partial(kernel, n_seq, n_kvh, size ** (-0.5)), o...  28.2 us
    pallas_call x1, Pallas kernels, step(): pl.pallas_call(finish, out_shape=shapes, in_specs=[anywhere] * 3, out_spe...  0.74 us

profile of v5, /device:TPU:1, one launch (start us, length us, event | category | flops | bytes accessed | tf_op | source)
XLA Modules:
  0.0 29.6 jit_solution(3453494946234736996)
XLA Ops:
  0.6 28.2 %shard_map.85 = (bf16[16,8,8,128]{3,2,1,0:T(8,128)(2,1)S(1)}, bf16[128,128]{1,0:T(8,128)(2,1)S(1)}, bf16[128,128]{1,0:T(8,128)(2,1)S(1)}) custom-call(bf16[128,8,128]{2,1,0:T(8,128)(2,1)} %q_hbm.1, bf16[128,128]{1,0:T(8,128)(2,1)} %bitcast.9, bf16[128,128]{1,0:T(8,128)(2,1)} %bitcast.10, bf16[16,8,8,128]{3,2,1,0:T(8,128)(2,1)} %bitcast.8, ...), custom_call_target="tpu_custom_call" | custom-call | tf_op jit(solution)/shard_map/pallas_call | solution.py:326
  28.9 0.7 %shard_map.86 = (bf16[16,8,8,128]{3,2,1,0:T(8,128)(2,1)}, bf16[128,128]{1,0:T(8,128)(2,1)}, bf16[128,128]{1,0:T(8,128)(2,1)}) custom-call(bf16[16,8,8,128]{3,2,1,0:T(8,128)(2,1)S(1)} %get-tuple-element.9.gq_in, bf16[128,128]{1,0:T(8,128)(2,1)S(1)} %get-tuple-element.10.gk_in, bf16[128,128]{1,0:T(8,128)(2,1)S(1)} %get-tuple-element.11.gv_in), custom_call_target="tpu_custom_call" | custom-call | tf_op jit(solution)/shard_map/pallas_call | solution.py:368

commit v6 on v5

--- a/solution.py
+++ b/solution.py
@@ -206,19 +206,23 @@
 
     local[4].wait()
     each_halo(-1, lambda number: halo_copy(1, number).wait_recv())
-    for k in range(n_kvh):
-        pltpu.make_async_copy(cot.at[k], cot.at[k], cot_recv.at[k]).wait()
-    for k in range(n_kvh):
-        block = cot[k].astype(jnp.float32).reshape(piece, -1)
-        c2[pl.ds(k * piece, piece), :] = block.astype(jnp.bfloat16)
-
-    order = (2, 1, 3, 0)
+    order = (0, 1, 3, 2)
     v_all = vbuf[...].reshape(TILES * tokens, -1)
     k_turned = jnp.transpose(k_all.astype(jnp.float32)).astype(jnp.bfloat16)
 
     def chunk_of(step):
         target = lax.rem(chip + order[step], chips)
         return target, pl.ds(pl.multiple_of(target * width, width), width)
+
+    def cotangents(step):
+        target, _ = chunk_of(step)
+        for core in (0, 1):
+            holder = 2 * target + core
+            pltpu.make_async_copy(cot.at[holder], cot.at[holder], cot_recv.at[holder]).wait()
+        for core in (0, 1):
+            holder = 2 * target + core
+            block = cot[holder].astype(jnp.float32).reshape(piece, -1)
+            c2[pl.ds(pl.multiple_of(holder * piece, piece), piece), :] = block.astype(jnp.bfloat16)
 
     def score_gradients(step):
         target, at = chunk_of(step)
@@ -261,15 +265,23 @@
             copy.start()
             queries.append(copy)
 
+    cotangents(0)
     ds_chunk = score_gradients(0)
-    store_parts(0, jnp.dot(probs_half[...], c2[...], preferred_element_type=jnp.float32))
-    send_parts(0)
-    key_total = None
-    for step in range(chips):
-        later = score_gradients(step + 1) if step + 1 < chips else None
+    query_gradients(0, ds_chunk)
+    key_total = key_gradients(0, ds_chunk)
+    send_queries(0)
+    cotangents(1)
+    ds_chunk = score_gradients(1)
+    for step in range(1, chips):
+        later = None
+        if step + 1 < chips:
+            cotangents(step + 1)
+            if step + 2 == chips:
+                store_parts(0, jnp.dot(probs_half[...], c2[...], preferred_element_type=jnp.float32))
+                send_parts(0)
+            later = score_gradients(step + 1)
         query_gradients(step, ds_chunk)
-        term = key_gradients(step, ds_chunk)
-        key_total = term if key_total is None else key_total + term
+        key_total = key_total + key_gradients(step, ds_chunk)
         if later is None:
             store_parts(1, key_total * scale)
             send_parts(1)

time: 29.8 us -> 30.5 us (1.023)
  Pallas kernels: 29 us -> 29.7 us
    pallas_call x1, Pallas kernels: 28.2 us -> 28.9 us  [step(): pl.pallas_call(functools.partial(kernel, n_seq, n_kvh, size ** (-0.5)), o...]
where the time goes in v6:
time: 30.5 us; the launch traced here: 30.3 us
  Pallas kernels  29.7 us (97%)
  between operations  0.64 us (2%)
    pallas_call x1, Pallas kernels, step(): pl.pallas_call(functools.partial(kernel, n_seq, n_kvh, size ** (-0.5)), o...  28.9 us
    pallas_call x1, Pallas kernels, step(): pl.pallas_call(finish, out_shape=shapes, in_specs=[anywhere] * 3, out_spe...  0.74 us

profile of v6, /device:TPU:1, one launch (start us, length us, event | category | flops | bytes accessed | tf_op | source)
XLA Modules:
  0.0 30.3 jit_solution(4600492525984111224)
XLA Ops:
  0.6 28.9 %shard_map.85 = (bf16[16,8,8,128]{3,2,1,0:T(8,128)(2,1)S(1)}, bf16[128,128]{1,0:T(8,128)(2,1)S(1)}, bf16[128,128]{1,0:T(8,128)(2,1)S(1)}) custom-call(bf16[128,8,128]{2,1,0:T(8,128)(2,1)} %q_hbm.1, bf16[128,128]{1,0:T(8,128)(2,1)} %bitcast.9, bf16[128,128]{1,0:T(8,128)(2,1)} %bitcast.10, bf16[16,8,8,128]{3,2,1,0:T(8,128)(2,1)} %bitcast.8, ...), custom_call_target="tpu_custom_call" | custom-call | tf_op jit(solution)/shard_map/pallas_call | solution.py:338
  29.6 0.7 %shard_map.86 = (bf16[16,8,8,128]{3,2,1,0:T(8,128)(2,1)}, bf16[128,128]{1,0:T(8,128)(2,1)}, bf16[128,128]{1,0:T(8,128)(2,1)}) custom-call(bf16[16,8,8,128]{3,2,1,0:T(8,128)(2,1)S(1)} %get-tuple-element.9.gq_in, bf16[128,128]{1,0:T(8,128)(2,1)S(1)} %get-tuple-element.10.gk_in, bf16[128,128]{1,0:T(8,128)(2,1)S(1)} %get-tuple-element.11.gv_in), custom_call_target="tpu_custom_call" | custom-call | tf_op jit(solution)/shard_map/pallas_call | solution.py:380

commit v7 on v5

--- a/solution.py
+++ b/solution.py
@@ -262,10 +262,11 @@
             queries.append(copy)
 
     ds_chunk = score_gradients(0)
-    store_parts(0, jnp.dot(probs_half[...], c2[...], preferred_element_type=jnp.float32))
-    send_parts(0)
     key_total = None
     for step in range(chips):
+        if step == 2:
+            store_parts(0, jnp.dot(probs_half[...], c2[...], preferred_element_type=jnp.float32))
+            send_parts(0)
         later = score_gradients(step + 1) if step + 1 < chips else None
         query_gradients(step, ds_chunk)
         term = key_gradients(step, ds_chunk)

time: 29.8 us -> 28.8 us (0.966)
  Pallas kernels: 29 us -> 28 us
    pallas_call x1, Pallas kernels: 28.2 us -> 27.3 us  [step(): pl.pallas_call(functools.partial(kernel, n_seq, n_kvh, size ** (-0.5)), o...]
where the time goes in v7:
time: 28.8 us; the launch traced here: 28.6 us
  Pallas kernels  28 us (97%)
  between operations  0.64 us (2%)
    pallas_call x1, Pallas kernels, step(): pl.pallas_call(functools.partial(kernel, n_seq, n_kvh, size ** (-0.5)), o...  27.3 us
    pallas_call x1, Pallas kernels, step(): pl.pallas_call(finish, out_shape=shapes, in_specs=[anywhere] * 3, out_spe...  0.74 us

profile of v7, /device:TPU:1, one launch (start us, length us, event | category | flops | bytes accessed | tf_op | source)
XLA Modules:
  0.0 28.6 jit_solution(16262206725184131151)
XLA Ops:
  0.6 27.3 %shard_map.85 = (bf16[16,8,8,128]{3,2,1,0:T(8,128)(2,1)S(1)}, bf16[128,128]{1,0:T(8,128)(2,1)S(1)}, bf16[128,128]{1,0:T(8,128)(2,1)S(1)}) custom-call(bf16[128,8,128]{2,1,0:T(8,128)(2,1)} %q_hbm.1, bf16[128,128]{1,0:T(8,128)(2,1)} %bitcast.9, bf16[128,128]{1,0:T(8,128)(2,1)} %bitcast.10, bf16[16,8,8,128]{3,2,1,0:T(8,128)(2,1)} %bitcast.8, ...), custom_call_target="tpu_custom_call" | custom-call | tf_op jit(solution)/shard_map/pallas_call | solution.py:327
  27.9 0.7 %shard_map.86 = (bf16[16,8,8,128]{3,2,1,0:T(8,128)(2,1)}, bf16[128,128]{1,0:T(8,128)(2,1)}, bf16[128,128]{1,0:T(8,128)(2,1)}) custom-call(bf16[16,8,8,128]{3,2,1,0:T(8,128)(2,1)S(1)} %get-tuple-element.9.gq_in, bf16[128,128]{1,0:T(8,128)(2,1)S(1)} %get-tuple-element.10.gk_in, bf16[128,128]{1,0:T(8,128)(2,1)S(1)} %get-tuple-element.11.gv_in), custom_call_target="tpu_custom_call" | custom-call | tf_op jit(solution)/shard_map/pallas_call | solution.py:369

commit v8 on v7

--- a/solution.py
+++ b/solution.py
@@ -196,10 +196,9 @@
         for slot, part in enumerate((before, middle, jnp.where(back, outer, 0.0), jnp.where(back, 0.0, outer))):
             probs_half[slot * tokens:(slot + 1) * tokens, at] = part.astype(jnp.bfloat16)
 
-    def store_parts(which, total):
-        for number, (_, slot) in enumerate(halo):
-            part_out[which, number] = total[slot * tokens:(slot + 1) * tokens].astype(jnp.bfloat16)
-        own[which] = total[OWN * tokens:(OWN + 1) * tokens]
+    def store_parts(which, before, outer):
+        for number, part in ((1, before), (0, outer[:tokens]), (2, outer[tokens:])):
+            part_out[which, number] = part.astype(jnp.bfloat16)
 
     def send_parts(which):
         each_halo(-1, lambda number: part_copy(which, number).start())
@@ -265,18 +264,24 @@
     key_total = None
     for step in range(chips):
         if step == 2:
-            store_parts(0, jnp.dot(probs_half[...], c2[...], preferred_element_type=jnp.float32))
+            store_parts(0, *(
+                jnp.dot(probs_half[rows_of, :], c2[...], preferred_element_type=jnp.float32)
+                for rows_of in (pl.ds(0, tokens), pl.ds(2 * tokens, 2 * tokens))
+            ))
             send_parts(0)
         later = score_gradients(step + 1) if step + 1 < chips else None
         query_gradients(step, ds_chunk)
         term = key_gradients(step, ds_chunk)
         key_total = term if key_total is None else key_total + term
         if later is None:
-            store_parts(1, key_total * scale)
+            key_total = key_total * scale
+            store_parts(1, key_total[:tokens], key_total[2 * tokens:])
+            own[1] = key_total[tokens:2 * tokens]
             send_parts(1)
         send_queries(step)
         ds_chunk = later
 
+    own[0] = jnp.dot(probs_half[OWN * tokens:(OWN + 1) * tokens, :], c2[...], preferred_element_type=jnp.float32)
     outs = []
     for which, out in ((0, gv_out), (1, gk_out)):
         total = own[which]

time: 28.8 us -> 29.1 us (1.010)
  Pallas kernels: 28 us -> 28.3 us
where the time goes in v8:
time: 29.1 us; the launch traced here: 28.9 us
  Pallas kernels  28.3 us (97%)
  between operations  0.64 us (2%)
    pallas_call x1, Pallas kernels, step(): pl.pallas_call(functools.partial(kernel, n_seq, n_kvh, size ** (-0.5)), o...  27.5 us
    pallas_call x1, Pallas kernels, step(): pl.pallas_call(finish, out_shape=shapes, in_specs=[anywhere] * 3, out_spe...  0.74 us

profile of v8, /device:TPU:1, one launch (start us, length us, event | category | flops | bytes accessed | tf_op | source)
XLA Modules:
  0.0 28.9 jit_solution(9431080336589076738)
XLA Ops:
  0.6 27.5 %shard_map.85 = (bf16[16,8,8,128]{3,2,1,0:T(8,128)(2,1)S(1)}, bf16[128,128]{1,0:T(8,128)(2,1)S(1)}, bf16[128,128]{1,0:T(8,128)(2,1)S(1)}) custom-call(bf16[128,8,128]{2,1,0:T(8,128)(2,1)} %q_hbm.1, bf16[128,128]{1,0:T(8,128)(2,1)} %bitcast.9, bf16[128,128]{1,0:T(8,128)(2,1)} %bitcast.10, bf16[16,8,8,128]{3,2,1,0:T(8,128)(2,1)} %bitcast.8, ...), custom_call_target="tpu_custom_call" | custom-call | tf_op jit(solution)/shard_map/pallas_call | solution.py:332
  28.2 0.7 %shard_map.86 = (bf16[16,8,8,128]{3,2,1,0:T(8,128)(2,1)}, bf16[128,128]{1,0:T(8,128)(2,1)}, bf16[128,128]{1,0:T(8,128)(2,1)}) custom-call(bf16[16,8,8,128]{3,2,1,0:T(8,128)(2,1)S(1)} %get-tuple-element.9.gq_in, bf16[128,128]{1,0:T(8,128)(2,1)S(1)} %get-tuple-element.10.gk_in, bf16[128,128]{1,0:T(8,128)(2,1)S(1)} %get-tuple-element.11.gv_in), custom_call_target="tpu_custom_call" | custom-call | tf_op jit(solution)/shard_map/pallas_call | solution.py:374
